TPU v7x, 32 devices: a whole 2x2x4 slice. The times are simulated.
32 devices in a mesh: rep: 8 (over y, x, core), shard: 4 (over z).
Axes of the slice: x: 2, y: 2, z: 4, core: 2. Of those that a mesh axis runs over, the one named last changes fastest.
Arguments:
- char_ids: int32 [128, 48], P(('rep', 'shard')), may hold values from 0 to 274
- prefix: int32 [128], P(('rep', 'shard')), may hold values from 4 to 24, as said below
- embedding: bfloat16 [2, 275, 100], replicated, may hold values from -6 to 6
- w_in: bfloat16 [2, 4, 100, 2048], P(None, None, None, 'shard'), may hold values from -0.625 to 0.625
- w_rec: bfloat16 [2, 4, 2048, 2048], P(None, None, None, 'shard'), may hold values from -0.125 to 0.125
- gate_bias: bfloat16 [2, 4, 2048], P(None, None, 'shard'), may hold values from -3 to 4
- w_out: bfloat16 [2, 2048, 275], P(None, 'shard'), may hold values from -0.875 to 0.875
- b_out: bfloat16 [2, 275], replicated, may hold values from -3 to 3
Outputs:
- grad_embed: float32 [2, 275, 100], replicated
- grad_in: float32 [2, 4, 100, 2048], P(None, None, None, 'shard')
- grad_rec: float32 [2, 4, 2048, 2048], P(None, None, 'rep', 'shard')
- grad_bias: float32 [2, 4, 2048], P(None, None, 'shard')
- grad_out: float32 [2, 2048, 275], P(None, 'shard')
- grad_bout: float32 [2, 275], replicated
Inputs may be any that keep to these rules, and one draw needn't show every extreme that they name: Some sequence has a prefix of exactly 24 characters.
All inputs are finite; a program needn't handle non-finite values.
Results may differ from a plain program's by a relative error of at most 0.0015.
Values may be sent and summed in bfloat16 or wider, within the bound.
A program may use at most 192 MiB of HBM per device.

v0:
```python
import math
import jax
import jax.numpy as jnp
from jax import lax
from jax.sharding import PartitionSpec as P

PRECISE = lax.Precision.HIGHEST


def one_hot(ids, width, out_type):
    return (ids[..., None] == jnp.arange(width, dtype=jnp.int32)).astype(out_type)


def loss_grad(logits, targets, active, factor):
    probabilities = jax.nn.softmax(logits, axis=-1)
    picked = one_hot(targets, logits.shape[-1], jnp.float32)
    return ((probabilities - picked) * (active * factor)[:, None]).astype(jnp.bfloat16)


def run_forward(projected, w_rec, start_pair, sender):

    def advance(state_pair, slot_proj):
        full_hidden, memory = state_pair
        gate_sum = slot_proj + jnp.einsum(
            "mbk,mgkn->mbgn", full_hidden, w_rec, preferred_element_type=jnp.float32
        )
        in_gate = jax.nn.sigmoid(gate_sum[..., 0, :])
        forget = jax.nn.sigmoid(gate_sum[..., 1, :])
        candidate = jnp.tanh(gate_sum[..., 2, :])
        out_gate = jax.nn.sigmoid(gate_sum[..., 3, :])
        new_memory = forget * memory + in_gate * candidate
        own_hidden = (out_gate * jnp.tanh(new_memory)).astype(jnp.bfloat16)
        new_full = sender(own_hidden)
        record = (
            jnp.stack([in_gate, forget, candidate, out_gate], axis=-2),
            new_memory,
            own_hidden,
            new_full,
        )
        return ((new_full, new_memory), record)

    return lax.scan(advance, start_pair, projected)


def run_backward(records, w_rec, start_pair, sender):

    def retreat(state_pair, record):
        from_later, cell_grad = state_pair
        gate_act, memory, prev_memory, from_decoder = record
        in_gate = gate_act[..., 0, :]
        forget = gate_act[..., 1, :]
        candidate = gate_act[..., 2, :]
        out_gate = gate_act[..., 3, :]
        grad_hidden = from_decoder + from_later
        squashed = jnp.tanh(memory)
        grad_memory = cell_grad + grad_hidden * out_gate * (1.0 - squashed * squashed)
        gate_grad = jnp.stack(
            [
                grad_memory * candidate * in_gate * (1.0 - in_gate),
                grad_memory * prev_memory * forget * (1.0 - forget),
                grad_memory * in_gate * (1.0 - candidate * candidate),
                grad_hidden * squashed * out_gate * (1.0 - out_gate),
            ],
            axis=-2,
        ).astype(jnp.bfloat16)
        partial_sum = jnp.einsum(
            "mbgn,mgkn->mbk", gate_grad, w_rec, preferred_element_type=jnp.float32
        )
        return ((sender(partial_sum), grad_memory * forget), gate_grad)

    return lax.scan(retreat, start_pair, records, reverse=True)


def shifted(values):
    return jnp.concatenate([jnp.zeros_like(values[:1]), values[:-1]], axis=0)


def shards(char_ids, prefix, embedding, w_in, w_rec, gate_bias, w_out, b_out):
    seq_dev, length = char_ids.shape
    half_len = length // 2
    vocab_size = embedding.shape[1]
    unit_count = w_rec.shape[2]
    shard_units = w_rec.shape[3]
    factor = 1.0 / math.sqrt(lax.axis_size("rep") * lax.axis_size("shard") * seq_dev * length)
    group_chars, group_prefix = (
        lax.all_gather(char_ids, "shard", axis=0, tiled=True),
        lax.all_gather(prefix, "shard", axis=0, tiled=True),
    )
    group_size = group_chars.shape[0]
    front_in = group_chars.T
    front_target = jnp.concatenate([group_chars[:, 1:], group_chars[:, :1]], axis=1).T
    timeline = jnp.arange(length, dtype=jnp.int32)[:, None]
    front_active = jnp.broadcast_to(
        (timeline < length - 1).astype(jnp.float32), (length, group_size)
    )
    reverse_steps = jnp.arange(half_len, dtype=jnp.int32)[:, None]
    back_in = jnp.take_along_axis(
        front_in, jnp.maximum(group_prefix[None, :] - 1 - reverse_steps, 0), axis=0
    )
    back_target = jnp.take_along_axis(
        front_in, jnp.maximum(group_prefix[None, :] - 2 - reverse_steps, 0), axis=0
    )
    back_active = (reverse_steps <= group_prefix[None, :] - 2).astype(jnp.float32)
    front_x = jnp.einsum(
        "tbv,ve->tbe",
        one_hot(front_in, vocab_size, jnp.bfloat16),
        embedding[0],
        preferred_element_type=jnp.float32,
    ).astype(jnp.bfloat16)
    back_x = jnp.einsum(
        "tbv,ve->tbe",
        one_hot(back_in, vocab_size, jnp.bfloat16),
        embedding[1],
        preferred_element_type=jnp.float32,
    ).astype(jnp.bfloat16)
    bias_wide = gate_bias.astype(jnp.float32)
    front_proj = (
        jnp.einsum("tbe,gen->tbgn", front_x, w_in[0], preferred_element_type=jnp.float32)
        + bias_wide[0]
    )
    back_proj = (
        jnp.einsum("tbe,gen->tbgn", back_x, w_in[1], preferred_element_type=jnp.float32)
        + bias_wide[1]
    )

    def move_both(own_hidden):
        return lax.all_gather(own_hidden, "shard", axis=2, tiled=True)

    def move_front(own_hidden):
        return lax.all_gather(own_hidden, "shard", axis=2, tiled=True)

    both_proj = jnp.stack([front_proj[:half_len], back_proj], axis=1)
    start_pair = (
        jnp.zeros((2, group_size, unit_count), jnp.bfloat16),
        jnp.zeros((2, group_size, shard_units), jnp.float32),
    )
    (mid_full, mid_memory), early_rec = run_forward(both_proj, w_rec, start_pair, move_both)
    front_weights = w_rec[:1]
    ignored, late_rec = run_forward(
        front_proj[half_len:, None], front_weights, (mid_full[:1], mid_memory[:1]), move_front
    )
    front_rec = tuple(
        (
            jnp.concatenate([head_part[:, :1], tail_part], axis=0)
            for head_part, tail_part in zip(early_rec, late_rec)
        )
    )
    back_rec = tuple((head_part[:, 1:] for head_part in early_rec))
    full_out = lax.all_gather(w_out, "shard", axis=1, tiled=True)
    first_seq = lax.axis_index("shard") * seq_dev
    front_rows = lax.dynamic_slice_in_dim(front_rec[3][:, 0], first_seq, seq_dev, axis=1).reshape(
        length * seq_dev, unit_count
    )
    back_rows = lax.dynamic_slice_in_dim(back_rec[3][:, 0], first_seq, seq_dev, axis=1).reshape(
        half_len * seq_dev, unit_count
    )
    own_front_target = lax.dynamic_slice_in_dim(front_target, first_seq, seq_dev, axis=1).reshape(
        -1
    )
    own_back_target = lax.dynamic_slice_in_dim(back_target, first_seq, seq_dev, axis=1).reshape(-1)
    own_front_active = lax.dynamic_slice_in_dim(front_active, first_seq, seq_dev, axis=1).reshape(
        -1
    )
    own_back_active = lax.dynamic_slice_in_dim(back_active, first_seq, seq_dev, axis=1).reshape(-1)
    front_logits = jnp.dot(front_rows, full_out[0], preferred_element_type=jnp.float32) + b_out[
        0
    ].astype(jnp.float32)
    back_logits = jnp.dot(back_rows, full_out[1], preferred_element_type=jnp.float32) + b_out[
        1
    ].astype(jnp.float32)
    front_grad = loss_grad(front_logits, own_front_target, own_front_active, factor)
    back_grad = loss_grad(back_logits, own_back_target, own_back_active, factor)
    front_part = jnp.einsum(
        "rv,kv->rk", front_grad, full_out[0], preferred_element_type=jnp.float32
    ).reshape(length, seq_dev, unit_count)
    back_part = jnp.einsum(
        "rv,kv->rk", back_grad, full_out[1], preferred_element_type=jnp.float32
    ).reshape(half_len, seq_dev, unit_count)
    front_dec, back_dec = (
        lax.all_to_all(front_part, "shard", split_axis=2, concat_axis=1, tiled=True),
        lax.all_to_all(back_part, "shard", split_axis=2, concat_axis=1, tiled=True),
    )
    front_dec = front_dec[:, None]
    back_dec = back_dec[:, None]
    out_whole = jnp.stack(
        [
            jnp.einsum("rk,rv->kv", front_rows, front_grad, preferred_element_type=jnp.float32),
            jnp.einsum("rk,rv->kv", back_rows, back_grad, preferred_element_type=jnp.float32),
        ]
    )
    out_grad = lax.psum_scatter(out_whole, "shard", scatter_dimension=1, tiled=True)
    bout_part = jnp.stack(
        [
            jnp.sum(front_grad, axis=0, dtype=jnp.float32),
            jnp.sum(back_grad, axis=0, dtype=jnp.float32),
        ]
    )

    def move_front_grad(partial_sum):
        return lax.psum_scatter(partial_sum, "shard", scatter_dimension=2, tiled=True)

    def move_both_grad(partial_sum):
        return lax.psum_scatter(partial_sum, "shard", scatter_dimension=2, tiled=True)

    front_prev_memory = shifted(front_rec[1])
    back_prev_memory = shifted(back_rec[1])
    blank_grad = jnp.zeros((1, group_size, shard_units), jnp.float32)
    late_records = (
        front_rec[0][half_len:],
        front_rec[1][half_len:],
        front_prev_memory[half_len:],
        front_dec[half_len:],
    )
    (carry_hidden, carry_memory), late_grads = run_backward(
        late_records, front_weights, (blank_grad, blank_grad), move_front_grad
    )
    prev_front = shifted(front_rec[3])[:, 0]
    prev_back = shifted(back_rec[3])[:, 0]
    early_records = (
        jnp.concatenate([front_rec[0][:half_len], back_rec[0]], axis=1),
        jnp.concatenate([front_rec[1][:half_len], back_rec[1]], axis=1),
        jnp.concatenate([front_prev_memory[:half_len], back_prev_memory], axis=1),
        jnp.concatenate([front_dec[:half_len], back_dec], axis=1),
    )
    start_back = (
        jnp.concatenate([carry_hidden, blank_grad], axis=0),
        jnp.concatenate([carry_memory, blank_grad], axis=0),
    )
    ignored, early_grads = run_backward(early_records, w_rec, start_back, move_both_grad)
    front_grads = jnp.concatenate([early_grads[:, :1], late_grads], axis=0)[:, 0]
    back_grads = early_grads[:, 1]
    front_rec_grad = jnp.einsum(
        "tbk,tbgn->gkn", prev_front, front_grads, preferred_element_type=jnp.float32
    )
    back_rec_grad = jnp.einsum(
        "tbk,tbgn->gkn", prev_back, back_grads, preferred_element_type=jnp.float32
    )
    rec_grad = lax.psum_scatter(
        jnp.stack([front_rec_grad, back_rec_grad]), "rep", scatter_dimension=2, tiled=True
    )
    in_grad = jnp.stack(
        [
            jnp.einsum("tbe,tbgn->gen", front_x, front_grads, preferred_element_type=jnp.float32),
            jnp.einsum("tbe,tbgn->gen", back_x, back_grads, preferred_element_type=jnp.float32),
        ]
    )
    bias_grad = jnp.stack(
        [
            jnp.sum(front_grads, axis=(0, 1), dtype=jnp.float32),
            jnp.sum(back_grads, axis=(0, 1), dtype=jnp.float32),
        ]
    )
    front_dx = jnp.einsum("tbgn,gen->tbe", front_grads, w_in[0], preferred_element_type=jnp.float32)
    back_dx = jnp.einsum("tbgn,gen->tbe", back_grads, w_in[1], preferred_element_type=jnp.float32)
    embed_grad = jnp.stack(
        [
            jnp.einsum(
                "tbv,tbe->ve",
                one_hot(front_in, vocab_size, jnp.float32),
                front_dx,
                precision=PRECISE,
            ),
            jnp.einsum(
                "tbv,tbe->ve", one_hot(back_in, vocab_size, jnp.float32), back_dx, precision=PRECISE
            ),
        ]
    )
    in_size = in_grad.size
    bias_size = bias_grad.size
    flat_grads = jnp.concatenate([in_grad.reshape(-1), bias_grad.reshape(-1), out_grad.reshape(-1)])
    summed_part = lax.psum_scatter(flat_grads, "rep", scatter_dimension=0, tiled=True)
    summed_flat = lax.all_gather(summed_part, "rep", axis=0, tiled=True)
    in_sum = summed_flat[:in_size].reshape(in_grad.shape)
    bias_sum = summed_flat[in_size : in_size + bias_size].reshape(bias_grad.shape)
    out_sum = summed_flat[in_size + bias_size :].reshape(out_grad.shape)
    embed_sum, bout_sum = lax.psum((embed_grad, bout_part), ("rep", "shard"))
    return (embed_sum, in_sum, rec_grad, bias_sum, out_sum, bout_sum)


def solution(mesh):
    in_specs = (
        P(("rep", "shard"), None),
        P(("rep", "shard")),
        P(),
        P(None, None, None, "shard"),
        P(None, None, None, "shard"),
        P(None, None, "shard"),
        P(None, "shard", None),
        P(),
    )
    out_specs = (
        P(),
        P(None, None, None, "shard"),
        P(None, None, "rep", "shard"),
        P(None, None, "shard"),
        P(None, "shard", None),
        P(),
    )
    return jax.shard_map(shards, mesh=mesh, in_specs=in_specs, out_specs=out_specs, check_vma=False)
```

profile of v0, /device:TPU:0, one launch (start us, length us, event | category | flops | bytes accessed | tf_op | source)
XLA Modules:
  0.0 3158.2 jit_solution(11104834085633158624)
XLA Ops:
  62.0 553.4 %while.76 = (s32[]{:T(128)}, bf16[2,16,2048]{2,1,0:T(8,128)(2,1)S(1)}, f32[2,16,512]{2,1,0:T(8,128)S(1)}, f32[24,2,16,4,512]{4,2,3,1,0:T(8,128)}, f32[24,2,16,51...) while((s32[]{:T(128)}, ...), condition=%wide.region_1.3_spmd.clone, body=%wide.region_0.2_spmd.clone.sunk | while | flops 269090816 | bytes 19464324 | solution.py:42
  616.6 474.4 %while.74 = (s32[]{:T(128)}, bf16[1,16,2048]{2,1,0:T(8,128)(2,1)S(1)}, f32[1,16,512]{2,1,0:T(8,128)S(1)}, f32[24,1,16,4,512]{4,2,3,1,0:T(8,128)}, f32[24,1,16,51...) while((s32[]{:T(128)}, ...), condition=%wide.region_3.5_spmd, body=%wide.region_2.4_spmd.sunk | while | flops 134537216 | bytes 9732213 | solution.py:42
  1205.7 637.4 %while.77 = (s32[]{:T(128)}, f32[1,16,512]{2,1,0:T(8,128)}, f32[1,16,512]{2,1,0:T(8,128)S(1)}, bf16[24,1,16,4,512]{4,2,3,1,0:T(8,128)(2,1)S(1)}, f32[24,1,16,512...) while((s32[]{:T(128)}, f32[1,16,512]{2,1,0:T(8,128)}, ...), condition=%wide.region_8.10_spmd.clone, body=%wide.region_6.9_spmd.clone.sunk | while | flops 134807552 | bytes 9961667 | solution.py:71
  1214.7 21.1 reduce-scatter.11.cloned.1.call-done
  1244.7 17.5 reduce-scatter.11.cloned.1.call-done
  1271.1 17.5 reduce-scatter.11.cloned.1.call-done
  1297.5 17.5 reduce-scatter.11.cloned.1.call-done
  1323.9 17.5 reduce-scatter.11.cloned.1.call-done
  1350.3 17.5 reduce-scatter.11.cloned.1.call-done
  1376.7 17.5 reduce-scatter.11.cloned.1.call-done
  1455.9 17.5 reduce-scatter.11.cloned.1.call-done
  1482.3 17.5 reduce-scatter.11.cloned.1.call-done
  1508.7 17.5 reduce-scatter.11.cloned.1.call-done
  1535.1 17.5 reduce-scatter.11.cloned.1.call-done
  1561.5 17.5 reduce-scatter.11.cloned.1.call-done
  1587.9 17.5 reduce-scatter.11.cloned.1.call-done
  1846.1 763.3 %while.75 = (s32[]{:T(128)}, f32[2,16,512]{2,1,0:T(8,128)}, f32[2,16,512]{2,1,0:T(8,128)S(1)}, bf16[24,2,16,4,512]{4,2,1,3,0:T(8,128)(2,1)S(1)}, f32[24,2,16,512...) while((s32[]{:T(128)}, f32[2,16,512]{2,1,0:T(8,128)}, ...), condition=%wide.region_13.15_spmd, body=%wide.region_11.14_spmd.sunk | while | flops 269598720 | bytes 19923120 | solution.py:71
  1860.0 18.0 reduce-scatter.9.cloned.1.call-done
  1891.7 18.0 reduce-scatter.9.cloned.1.call-done
  1923.5 18.0 reduce-scatter.9.cloned.1.call-done
  1955.3 18.0 reduce-scatter.9.cloned.1.call-done
  1987.1 18.0 reduce-scatter.9.cloned.1.call-done
  2018.9 18.0 reduce-scatter.9.cloned.1.call-done
  2050.7 18.0 reduce-scatter.9.cloned.1.call-done
  2082.5 18.0 reduce-scatter.9.cloned.1.call-done
  2114.3 18.0 reduce-scatter.9.cloned.1.call-done
  2146.1 18.0 reduce-scatter.9.cloned.1.call-done
  2177.9 18.0 reduce-scatter.9.cloned.1.call-done
  2209.7 18.0 reduce-scatter.9.cloned.1.call-done
  2241.5 18.0 reduce-scatter.9.cloned.1.call-done
  2273.3 18.0 reduce-scatter.9.cloned.1.call-done
  2305.1 18.0 reduce-scatter.9.cloned.1.call-done
  2337.0 18.1 reduce-scatter.9.cloned.1.call-done
  2368.8 18.0 reduce-scatter.9.cloned.1.call-done
  2400.6 18.0 reduce-scatter.9.cloned.1.call-done
  2432.4 18.0 reduce-scatter.9.cloned.1.call-done
  2464.2 18.0 reduce-scatter.9.cloned.1.call-done
  2496.0 18.0 reduce-scatter.9.cloned.1.call-done
  2527.8 18.0 reduce-scatter.9.cloned.1.call-done
  2559.6 18.0 reduce-scatter.9.cloned.1.call-done
  2591.4 18.0 reduce-scatter.9.cloned.1.call-done
  2623.7 70.3 %reduce-scatter.5.cloned.1.call-done = f32[2,512,275]{1,2,0:T(8,128)} async-done(((f32[2,2048,275]{1,2,0:T(8,128)}), f32[2,512,275]{1,2,0:T(8,128)}) %reduce-scatter.5.cloned.1.call-update) | async-done | bytes 1126416 | tf_op jit(solution)/shard_map/reduce_scatter | solution.py:191
  2714.3 57.1 %all-reduce.13.cloned.1.call-done = f32[695296]{0:T(1024)} async-done(((f32[695296]{0:T(1024)}), f32[695296]{0:T(1024)}) %all-reduce.13.cloned.1.call-update) | async-done | bytes 2781200
  2791.5 19.1 pad_maximum_fusion
  2811.3 39.5 %psum.15 = f32[2,275]{1,0:T(2,128)} all-reduce(f32[2,275]{1,0:T(2,128)S(1)} %pad_maximum_fusion.7), channel_id=1, replica_groups=mesh['rep'=8,'shard'=4] {'rep','shard'}, use_global_device_ids=true, to_apply=%region_22.24 | all-reduce | flops 550 | bytes 4400 | tf_op jit(solution)/shard_map/psum | solution.py:276
  2850.8 52.2 %all-reduce.11.cloned.1.call-done = f32[2,275,100]{2,1,0:T(8,128)} async-done(((f32[2,275,100]{2,1,0:T(8,128)}), f32[2,275,100]{2,1,0:T(8,128)}) %all-reduce.11.cloned.1.call-update) | async-done | bytes 220016 | tf_op jit(solution)/shard_map/psum | solution.py:276
  2904.8 32.3 %all-gather.7.cloned.1.call-done = f32[8,1,86912]{2,1,0:T(1,128)} async-done(((f32[1,1,86912]{2,1,0:T(1,128)}), f32[8,1,86912]{2,1,0:T(1,128)}) %all-gather.7.cloned.1.call-update) | async-done | bytes 2781200 | tf_op jit(solution)/shard_map/all_gather | solution.py:272
  2947.7 198.2 %reduce-scatter.7.cloned.1.call-done = f32[2,4,256,512]{2,3,1,0:T(8,128)} async-done(((f32[2,4,2048,512]{2,3,1,0:T(8,128)}), f32[2,4,256,512]{2,3,1,0:T(8,128)}) %reduce-scatter.7.cloned.1.call-update) | async-done | bytes 4194320 | tf_op jit(solution)/shard_map/reduce_scatter | solution.py:238
  (940 shorter events, 2007.4 us)
Async XLA Ops:
  7.2 1101.7 %all-gather.5.cloned.1.call-start = ((), (), s32[]{:S(2)}) async-start(), calls=%async_computation.6 | async-start | bytes 2867200 | tf_op jit(solution)/shard_map/all_gather | solution.py:149
  1144.9 30.4 all-to-all-start
  1205.7 30.1 reduce-scatter.11.cloned.1.call-start
  1235.8 26.4 reduce-scatter.11.cloned.1.call-start
  1262.2 26.4 reduce-scatter.11.cloned.1.call-start
  1288.6 26.4 reduce-scatter.11.cloned.1.call-start
  1315.0 26.4 reduce-scatter.11.cloned.1.call-start
  1341.4 26.4 reduce-scatter.11.cloned.1.call-start
  1367.8 26.4 reduce-scatter.11.cloned.1.call-start
  1394.2 26.4 reduce-scatter.11.cloned.1.call-start
  1499.8 26.4 reduce-scatter.11.cloned.1.call-start
  1526.2 26.4 reduce-scatter.11.cloned.1.call-start
  1552.6 26.4 reduce-scatter.11.cloned.1.call-start
  1579.0 26.4 reduce-scatter.11.cloned.1.call-start
  1605.4 26.4 reduce-scatter.11.cloned.1.call-start
  1631.8 26.4 reduce-scatter.11.cloned.1.call-start
  1763.8 26.4 reduce-scatter.11.cloned.1.call-start
  1790.2 26.4 reduce-scatter.11.cloned.1.call-start
  1816.6 26.4 reduce-scatter.11.cloned.1.call-start
  1846.1 31.8 %reduce-scatter.9.cloned.1.call-start = ((), (), s32[]{:S(2)}) async-start(), calls=%async_computation.12 | async-start | bytes 327680 | tf_op jit(solution)/shard_map/while/body/eval_jaxpr/reduce_scatter | solution.py:203
  1877.9 31.8 %reduce-scatter.9.cloned.1.call-start = ((), (), s32[]{:S(2)}) async-start(), calls=%async_computation.12 | async-start | bytes 327680 | tf_op jit(solution)/shard_map/while/body/eval_jaxpr/reduce_scatter | solution.py:203
  1909.7 31.8 %reduce-scatter.9.cloned.1.call-start = ((), (), s32[]{:S(2)}) async-start(), calls=%async_computation.12 | async-start | bytes 327680 | tf_op jit(solution)/shard_map/while/body/eval_jaxpr/reduce_scatter | solution.py:203
  1941.5 31.8 %reduce-scatter.9.cloned.1.call-start = ((), (), s32[]{:S(2)}) async-start(), calls=%async_computation.12 | async-start | bytes 327680 | tf_op jit(solution)/shard_map/while/body/eval_jaxpr/reduce_scatter | solution.py:203
  1973.3 31.8 %reduce-scatter.9.cloned.1.call-start = ((), (), s32[]{:S(2)}) async-start(), calls=%async_computation.12 | async-start | bytes 327680 | tf_op jit(solution)/shard_map/while/body/eval_jaxpr/reduce_scatter | solution.py:203
  2005.1 31.8 %reduce-scatter.9.cloned.1.call-start = ((), (), s32[]{:S(2)}) async-start(), calls=%async_computation.12 | async-start | bytes 327680 | tf_op jit(solution)/shard_map/while/body/eval_jaxpr/reduce_scatter | solution.py:203
  2036.9 31.8 %reduce-scatter.9.cloned.1.call-start = ((), (), s32[]{:S(2)}) async-start(), calls=%async_computation.12 | async-start | bytes 327680 | tf_op jit(solution)/shard_map/while/body/eval_jaxpr/reduce_scatter | solution.py:203
  2068.7 31.8 %reduce-scatter.9.cloned.1.call-start = ((), (), s32[]{:S(2)}) async-start(), calls=%async_computation.12 | async-start | bytes 327680 | tf_op jit(solution)/shard_map/while/body/eval_jaxpr/reduce_scatter | solution.py:203
  2100.5 31.8 %reduce-scatter.9.cloned.1.call-start = ((), (), s32[]{:S(2)}) async-start(), calls=%async_computation.12 | async-start | bytes 327680 | tf_op jit(solution)/shard_map/while/body/eval_jaxpr/reduce_scatter | solution.py:203
  2132.3 31.8 %reduce-scatter.9.cloned.1.call-start = ((), (), s32[]{:S(2)}) async-start(), calls=%async_computation.12 | async-start | bytes 327680 | tf_op jit(solution)/shard_map/while/body/eval_jaxpr/reduce_scatter | solution.py:203
  2164.1 31.8 %reduce-scatter.9.cloned.1.call-start = ((), (), s32[]{:S(2)}) async-start(), calls=%async_computation.12 | async-start | bytes 327680 | tf_op jit(solution)/shard_map/while/body/eval_jaxpr/reduce_scatter | solution.py:203
  2195.9 31.8 %reduce-scatter.9.cloned.1.call-start = ((), (), s32[]{:S(2)}) async-start(), calls=%async_computation.12 | async-start | bytes 327680 | tf_op jit(solution)/shard_map/while/body/eval_jaxpr/reduce_scatter | solution.py:203
  2227.7 31.8 %reduce-scatter.9.cloned.1.call-start = ((), (), s32[]{:S(2)}) async-start(), calls=%async_computation.12 | async-start | bytes 327680 | tf_op jit(solution)/shard_map/while/body/eval_jaxpr/reduce_scatter | solution.py:203
  2259.6 31.8 %reduce-scatter.9.cloned.1.call-start = ((), (), s32[]{:S(2)}) async-start(), calls=%async_computation.12 | async-start | bytes 327680 | tf_op jit(solution)/shard_map/while/body/eval_jaxpr/reduce_scatter | solution.py:203
  2291.4 31.8 %reduce-scatter.9.cloned.1.call-start = ((), (), s32[]{:S(2)}) async-start(), calls=%async_computation.12 | async-start | bytes 327680 | tf_op jit(solution)/shard_map/while/body/eval_jaxpr/reduce_scatter | solution.py:203
  2323.2 31.8 %reduce-scatter.9.cloned.1.call-start = ((), (), s32[]{:S(2)}) async-start(), calls=%async_computation.12 | async-start | bytes 327680 | tf_op jit(solution)/shard_map/while/body/eval_jaxpr/reduce_scatter | solution.py:203
  2355.0 31.8 %reduce-scatter.9.cloned.1.call-start = ((), (), s32[]{:S(2)}) async-start(), calls=%async_computation.12 | async-start | bytes 327680 | tf_op jit(solution)/shard_map/while/body/eval_jaxpr/reduce_scatter | solution.py:203
  2386.8 31.8 %reduce-scatter.9.cloned.1.call-start = ((), (), s32[]{:S(2)}) async-start(), calls=%async_computation.12 | async-start | bytes 327680 | tf_op jit(solution)/shard_map/while/body/eval_jaxpr/reduce_scatter | solution.py:203
  2418.6 31.8 %reduce-scatter.9.cloned.1.call-start = ((), (), s32[]{:S(2)}) async-start(), calls=%async_computation.12 | async-start | bytes 327680 | tf_op jit(solution)/shard_map/while/body/eval_jaxpr/reduce_scatter | solution.py:203
  2450.4 31.8 %reduce-scatter.9.cloned.1.call-start = ((), (), s32[]{:S(2)}) async-start(), calls=%async_computation.12 | async-start | bytes 327680 | tf_op jit(solution)/shard_map/while/body/eval_jaxpr/reduce_scatter | solution.py:203
  2482.2 31.8 %reduce-scatter.9.cloned.1.call-start = ((), (), s32[]{:S(2)}) async-start(), calls=%async_computation.12 | async-start | bytes 327680 | tf_op jit(solution)/shard_map/while/body/eval_jaxpr/reduce_scatter | solution.py:203
  2514.0 31.8 %reduce-scatter.9.cloned.1.call-start = ((), (), s32[]{:S(2)}) async-start(), calls=%async_computation.12 | async-start | bytes 327680 | tf_op jit(solution)/shard_map/while/body/eval_jaxpr/reduce_scatter | solution.py:203
  2545.8 31.8 %reduce-scatter.9.cloned.1.call-start = ((), (), s32[]{:S(2)}) async-start(), calls=%async_computation.12 | async-start | bytes 327680 | tf_op jit(solution)/shard_map/while/body/eval_jaxpr/reduce_scatter | solution.py:203
  2577.6 31.8 %reduce-scatter.9.cloned.1.call-start = ((), (), s32[]{:S(2)}) async-start(), calls=%async_computation.12 | async-start | bytes 327680 | tf_op jit(solution)/shard_map/while/body/eval_jaxpr/reduce_scatter | solution.py:203
  2609.4 84.6 %reduce-scatter.5.cloned.1.call-start = ((), (), s32[]{:S(2)}) async-start(), calls=%async_computation.8 | async-start | bytes 5734400 | tf_op jit(solution)/shard_map/reduce_scatter | solution.py:191
  2610.2 161.2 %all-reduce.13.cloned.1.call-start = ((), (), s32[]{:S(2)}) async-start(), calls=%async_computation.11 | async-start | bytes 5562368
  2704.2 198.8 %all-reduce.11.cloned.1.call-start = ((), (), s32[]{:S(2)}) async-start(), calls=%async_computation.7 | async-start | bytes 573440 | tf_op jit(solution)/shard_map/psum | solution.py:276
  2710.2 226.8 %all-gather.7.cloned.1.call-start = ((), (), s32[]{:S(2)}) async-start(), calls=%async_computation.10 | async-start | bytes 3128832 | tf_op jit(solution)/shard_map/all_gather | solution.py:272
  2773.5 372.4 %reduce-scatter.7.cloned.1.call-start = ((), (), s32[]{:S(2)}) async-start(), calls=%async_computation.9 | async-start | bytes 37748736 | tf_op jit(solution)/shard_map/reduce_scatter | solution.py:238
  (45 other events, 1454.6 us)
Sparse Core Ops, SparseCore 0:
  9.6 52.1 all-gather.4
  1214.8 20.9 reduce-scatter.10
  1244.8 17.3 reduce-scatter.10
  1271.2 17.3 reduce-scatter.10
  1297.6 17.3 reduce-scatter.10
  1324.0 17.3 reduce-scatter.10
  1350.4 17.3 reduce-scatter.10
  1376.8 17.3 reduce-scatter.10
  1403.2 17.3 reduce-scatter.10
  1429.6 17.3 reduce-scatter.10
  1456.0 17.3 reduce-scatter.10
  1482.4 17.3 reduce-scatter.10
  1508.8 17.3 reduce-scatter.10
  1535.2 17.3 reduce-scatter.10
  1561.6 17.3 reduce-scatter.10
  1588.0 17.3 reduce-scatter.10
  1614.4 17.3 reduce-scatter.10
  1640.8 17.3 reduce-scatter.10
  1667.2 17.3 reduce-scatter.10
  1860.1 17.8 reduce-scatter.8
  1891.8 17.8 reduce-scatter.8
  1923.6 17.8 reduce-scatter.8
  1955.4 17.8 reduce-scatter.8
  1987.2 17.8 reduce-scatter.8
  2019.0 17.8 reduce-scatter.8
  2050.8 17.8 reduce-scatter.8
  2082.6 17.8 reduce-scatter.8
  2114.4 17.8 reduce-scatter.8
  2146.2 17.8 reduce-scatter.8
  2178.0 17.8 reduce-scatter.8
  2209.8 17.8 reduce-scatter.8
  2241.6 17.8 reduce-scatter.8
  2273.4 17.8 reduce-scatter.8
  2305.2 17.8 reduce-scatter.8
  2337.0 17.9 reduce-scatter.8
  2368.9 17.8 reduce-scatter.8
  2400.7 17.8 reduce-scatter.8
  2432.5 17.8 reduce-scatter.8
  2464.3 17.8 reduce-scatter.8
  2496.1 17.8 reduce-scatter.8
  2527.9 17.8 reduce-scatter.8
  2559.7 17.8 reduce-scatter.8
  2591.5 17.8 reduce-scatter.8
  2612.6 81.3 reduce-scatter.4
  2704.3 67.0 all-reduce.12
  2777.6 125.3 all-reduce.10
  2905.3 31.7 all-gather.6
  2940.6 205.2 reduce-scatter.6
  (6 shorter events, 103.9 us)
where the time goes:
time: 3180 us; the launch traced here: 3160 us
  waiting for transfers between devices  1270 us (40%)
  matrix products  753 us (24%)
  blocking collectives  700 us (22%)
  local copies, waits for them, and re-layouts  205 us (6%)
  other arithmetic  204 us (6%)
    reduce_scatter x24, waiting for transfers between devices, move_both_grad(): lax.psum_scatter(partial_sum, 'shard', scatter_dimension=2, tiled=True)  432 us
    reduce_scatter x24, waiting for transfers between devices, move_front_grad(): lax.psum_scatter(partial_sum, 'shard', scatter_dimension=2, tiled=True)  424 us
    dot_general x48, matrix products, retreat(): jnp.einsum('mbgn,mgkn->mbk', gate_grad, w_rec, preferred_element_type=jnp...  413 us
    all_gather x24, blocking collectives, move_both(): return lax.all_gather(own_hidden, 'shard', axis=2, tiled=True)  322 us
    all_gather x24, blocking collectives, move_front(): return lax.all_gather(own_hidden, 'shard', axis=2, tiled=True)  316 us
    dot_general x48, matrix products, advance(): jnp.einsum('mbk,mgkn->mbgn', full_hidden, w_rec, preferred_element_type=j...  303 us
    reduce_scatter x1, waiting for transfers between devices, shards(): lax.psum_scatter(jnp.stack([front_rec_grad, back_rec_grad]), 'rep', scatt...  198 us
    reduce_scatter x1, waiting for transfers between devices, shards(): lax.psum_scatter(out_whole, 'shard', scatter_dimension=1, tiled=True)  70.3 us
  transfers between devices with their start and end apart: 56, of which 53 were waited for; matrix products, arithmetic and copies ran while one was open for 17% of the time, Pallas kernels for 0%

commit v1 on v0

--- a/solution.py
+++ b/solution.py
@@ -127,7 +127,22 @@
         return lax.all_gather(own_hidden, "shard", axis=2, tiled=True)
 
     def move_front(own_hidden):
-        return lax.all_gather(own_hidden, "shard", axis=2, tiled=True)
+
+        def lay_the_tables(raw):
+            lane_axis = "shard"
+            response = lax.axis_size(lane_axis)
+            base_arr = lax.axis_index(lane_axis)
+            everything, near, v_now = (response, base_arr, raw.shape[2])
+            all_values, arr_next = (raw, 1)
+            while arr_next < everything:
+                z2 = tuple(((num, (num - arr_next) % everything) for num in range(everything)))
+                seen_now = lax.ppermute(all_values, axis_name=lane_axis, perm=z2)
+                all_values = jnp.concatenate([all_values, seen_now], 2)
+                arr_next = 2 * arr_next
+            y2 = jnp.roll(all_values, near * v_now, 2)
+            return y2
+
+        return lay_the_tables(own_hidden)
 
     both_proj = jnp.stack([front_proj[:half_len], back_proj], axis=1)
     start_pair = (

time: 3180 us -> 3080 us (0.969)
  blocking collectives: 700 us -> 384 us
  waiting for transfers between devices: 1270 us -> 1390 us
  starting transfers between devices: 10.5 us -> 126 us
    all_gather x24 -> x0, blocking collectives: 316 us -> none  [move_front(): return lax.all_gather(own_hidden, 'shard', axis=2, tiled=True)]
    ppermute x0 -> x48, waiting for transfers between devices: none -> 118 us  [lay_the_tables(): seen_now = lax.ppermute(all_values, axis_name=lane_axis, perm=z2)]
    ppermute x0 -> x48, starting transfers between devices: none -> 115 us  [lay_the_tables(): seen_now = lax.ppermute(all_values, axis_name=lane_axis, perm=z2)]
  transfers between devices with their start and end apart: 56 -> 104, of which waited for: 53 -> 101; matrix products, arithmetic and copies ran while one was open for 17% -> 17% of each run, Pallas kernels for 0% -> 0%
where the time goes in v1:
time: 3080 us; the launch traced here: 3060 us
  waiting for transfers between devices  1390 us (45%)
  matrix products  752 us (24%)
  blocking collectives  384 us (12%)
  local copies, waits for them, and re-layouts  207 us (7%)
  other arithmetic  188 us (6%)
  starting transfers between devices  126 us (4%)
    reduce_scatter x24, waiting for transfers between devices, move_both_grad(): lax.psum_scatter(partial_sum, 'shard', scatter_dimension=2, tiled=True)  432 us
    reduce_scatter x24, waiting for transfers between devices, move_front_grad(): lax.psum_scatter(partial_sum, 'shard', scatter_dimension=2, tiled=True)  424 us
    dot_general x48, matrix products, retreat(): jnp.einsum('mbgn,mgkn->mbk', gate_grad, w_rec, preferred_element_type=jnp...  413 us
    all_gather x24, blocking collectives, move_both(): return lax.all_gather(own_hidden, 'shard', axis=2, tiled=True)  323 us
    dot_general x48, matrix products, advance(): jnp.einsum('mbk,mgkn->mbgn', full_hidden, w_rec, preferred_element_type=j...  303 us
    reduce_scatter x1, waiting for transfers between devices, shards(): lax.psum_scatter(jnp.stack([front_rec_grad, back_rec_grad]), 'rep', scatt...  198 us
    ppermute x48, waiting for transfers between devices, lay_the_tables(): seen_now = lax.ppermute(all_values, axis_name=lane_axis, perm=z2)  118 us
    ppermute x48, starting transfers between devices, lay_the_tables(): seen_now = lax.ppermute(all_values, axis_name=lane_axis, perm=z2)  115 us
  transfers between devices with their start and end apart: 104, of which 101 were waited for; matrix products, arithmetic and copies ran while one was open for 17% of the time, Pallas kernels for 0%

profile of v1, /device:TPU:0, one launch (start us, length us, event | category | flops | bytes accessed | tf_op | source)
XLA Modules:
  0.0 3063.8 jit_solution(11676688708307208961)
XLA Ops:
  50.9 554.0 %while.78 = (s32[]{:T(128)}, bf16[2,16,2048]{2,1,0:T(8,128)(2,1)S(1)}, f32[2,16,512]{2,1,0:T(8,128)S(1)}, f32[24,2,16,4,512]{4,2,3,1,0:T(8,128)}, f32[24,2,16,51...) while((s32[]{:T(128)}, ...), condition=%wide.region_1.3_spmd.clone, body=%wide.region_0.2_spmd.clone.sunk | while | flops 269090816 | bytes 19464324 | solution.py:42
  630.1 378.4 %while.76 = (s32[]{:T(128)}, bf16[1,16,2048]{2,1,0:T(8,128)(2,1)S(1)}, f32[1,16,512]{2,1,0:T(8,128)S(1)}, f32[24,1,16,4,512]{4,2,3,1,0:T(8,128)}, f32[24,1,16,51...) while((s32[]{:T(128)}, ...), condition=%wide.region_3.5_spmd, body=%wide.region_2.4_spmd.sunk | while | flops 134602752 | bytes 10224052 | solution.py:42
  1111.4 637.2 %while.79 = (s32[]{:T(128)}, f32[1,16,512]{2,1,0:T(8,128)}, f32[1,16,512]{2,1,0:T(8,128)S(1)}, bf16[24,1,16,4,512]{4,2,3,1,0:T(8,128)(2,1)S(1)}, f32[24,1,16,512...) while((s32[]{:T(128)}, f32[1,16,512]{2,1,0:T(8,128)}, ...), condition=%wide.region_8.10_spmd.clone, body=%wide.region_6.9_spmd.clone.sunk | while | flops 134807552 | bytes 9961667 | solution.py:71
  1120.5 20.9 reduce-scatter.11.cloned.1.call-done
  1203.0 17.5 reduce-scatter.11.cloned.1.call-done
  1229.4 17.5 reduce-scatter.11.cloned.1.call-done
  1255.8 17.5 reduce-scatter.11.cloned.1.call-done
  1282.2 17.5 reduce-scatter.11.cloned.1.call-done
  1308.6 17.5 reduce-scatter.11.cloned.1.call-done
  1335.1 17.5 reduce-scatter.11.cloned.1.call-done
  1361.5 17.5 reduce-scatter.11.cloned.1.call-done
  1440.7 17.5 reduce-scatter.11.cloned.1.call-done
  1467.1 17.5 reduce-scatter.11.cloned.1.call-done
  1493.5 17.5 reduce-scatter.11.cloned.1.call-done
  1519.9 17.5 reduce-scatter.11.cloned.1.call-done
  1546.3 17.5 reduce-scatter.11.cloned.1.call-done
  1751.7 763.4 %while.77 = (s32[]{:T(128)}, f32[2,16,512]{2,1,0:T(8,128)}, f32[2,16,512]{2,1,0:T(8,128)S(1)}, bf16[24,2,16,4,512]{4,2,1,3,0:T(8,128)(2,1)S(1)}, f32[24,2,16,512...) while((s32[]{:T(128)}, f32[2,16,512]{2,1,0:T(8,128)}, ...), condition=%wide.region_13.15_spmd, body=%wide.region_11.14_spmd.sunk | while | flops 269598720 | bytes 19923120 | solution.py:71
  1765.6 17.9 reduce-scatter.9.cloned.1.call-done
  1797.2 18.0 reduce-scatter.9.cloned.1.call-done
  1829.0 18.0 reduce-scatter.9.cloned.1.call-done
  1860.8 18.0 reduce-scatter.9.cloned.1.call-done
  1892.6 18.0 reduce-scatter.9.cloned.1.call-done
  1924.4 18.0 reduce-scatter.9.cloned.1.call-done
  1956.2 18.0 reduce-scatter.9.cloned.1.call-done
  1988.0 18.1 reduce-scatter.9.cloned.1.call-done
  2019.9 18.0 reduce-scatter.9.cloned.1.call-done
  2051.7 18.0 reduce-scatter.9.cloned.1.call-done
  2083.5 18.0 reduce-scatter.9.cloned.1.call-done
  2115.3 18.0 reduce-scatter.9.cloned.1.call-done
  2147.1 18.1 reduce-scatter.9.cloned.1.call-done
  2179.0 18.0 reduce-scatter.9.cloned.1.call-done
  2210.8 18.0 reduce-scatter.9.cloned.1.call-done
  2242.6 18.0 reduce-scatter.9.cloned.1.call-done
  2274.4 18.0 reduce-scatter.9.cloned.1.call-done
  2306.2 18.0 reduce-scatter.9.cloned.1.call-done
  2338.0 18.0 reduce-scatter.9.cloned.1.call-done
  2369.8 18.0 reduce-scatter.9.cloned.1.call-done
  2401.6 18.0 reduce-scatter.9.cloned.1.call-done
  2433.4 18.0 reduce-scatter.9.cloned.1.call-done
  2465.2 18.0 reduce-scatter.9.cloned.1.call-done
  2497.0 18.0 reduce-scatter.9.cloned.1.call-done
  2529.3 70.3 %reduce-scatter.5.cloned.1.call-done = f32[2,512,275]{1,2,0:T(8,128)} async-done(((f32[2,2048,275]{1,2,0:T(8,128)}), f32[2,512,275]{1,2,0:T(8,128)}) %reduce-scatter.5.cloned.1.call-update) | async-done | bytes 1126416 | tf_op jit(solution)/shard_map/reduce_scatter | solution.py:206
  2619.9 57.1 %all-reduce.13.cloned.1.call-done = f32[695296]{0:T(1024)} async-done(((f32[695296]{0:T(1024)}), f32[695296]{0:T(1024)}) %all-reduce.13.cloned.1.call-update) | async-done | bytes 2781200
  2697.2 19.1 pad_maximum_fusion.1
  2717.0 39.5 %psum.15 = f32[2,275]{1,0:T(2,128)} all-reduce(f32[2,275]{1,0:T(2,128)S(1)} %pad_maximum_fusion.8), channel_id=1, replica_groups=mesh['rep'=8,'shard'=4] {'rep','shard'}, use_global_device_ids=true, to_apply=%region_22.24 | all-reduce | flops 550 | bytes 4400 | tf_op jit(solution)/shard_map/psum | solution.py:291
  2756.5 52.1 %all-reduce.11.cloned.1.call-done = f32[2,275,100]{2,1,0:T(8,128)} async-done(((f32[2,275,100]{2,1,0:T(8,128)}), f32[2,275,100]{2,1,0:T(8,128)}) %all-reduce.11.cloned.1.call-update) | async-done | bytes 220016 | tf_op jit(solution)/shard_map/psum | solution.py:291
  2810.4 32.3 %all-gather.7.cloned.1.call-done = f32[8,1,86912]{2,1,0:T(1,128)} async-done(((f32[1,1,86912]{2,1,0:T(1,128)}), f32[8,1,86912]{2,1,0:T(1,128)}) %all-gather.7.cloned.1.call-update) | async-done | bytes 2781200 | tf_op jit(solution)/shard_map/all_gather | solution.py:287
  2853.3 198.2 %reduce-scatter.7.cloned.1.call-done = f32[2,4,256,512]{2,3,1,0:T(8,128)} async-done(((f32[2,4,2048,512]{2,3,1,0:T(8,128)}), f32[2,4,256,512]{2,3,1,0:T(8,128)}) %reduce-scatter.7.cloned.1.call-update) | async-done | bytes 4194320 | tf_op jit(solution)/shard_map/reduce_scatter | solution.py:253
  (1158 shorter events, 1912.2 us)
Async XLA Ops:
  7.2 1004.7 %all-gather.5.cloned.1.call-start = ((), (), s32[]{:S(2)}) async-start(), calls=%async_computation.6 | async-start | bytes 2867200 | tf_op jit(solution)/shard_map/all_gather | solution.py:164
  1050.6 30.4 all-to-all-start
  1111.5 29.9 reduce-scatter.11.cloned.1.call-start
  1167.7 26.4 reduce-scatter.11.cloned.1.call-start
  1194.1 26.4 reduce-scatter.11.cloned.1.call-start
  1220.5 26.4 reduce-scatter.11.cloned.1.call-start
  1246.9 26.4 reduce-scatter.11.cloned.1.call-start
  1273.3 26.4 reduce-scatter.11.cloned.1.call-start
  1299.8 26.4 reduce-scatter.11.cloned.1.call-start
  1326.2 26.4 reduce-scatter.11.cloned.1.call-start
  1352.6 26.4 reduce-scatter.11.cloned.1.call-start
  1379.0 26.4 reduce-scatter.11.cloned.1.call-start
  1405.4 26.4 reduce-scatter.11.cloned.1.call-start
  1484.6 26.4 reduce-scatter.11.cloned.1.call-start
  1511.0 26.4 reduce-scatter.11.cloned.1.call-start
  1537.4 26.4 reduce-scatter.11.cloned.1.call-start
  1563.8 26.4 reduce-scatter.11.cloned.1.call-start
  1590.2 26.4 reduce-scatter.11.cloned.1.call-start
  1616.6 26.4 reduce-scatter.11.cloned.1.call-start
  1751.7 31.8 %reduce-scatter.9.cloned.1.call-start = ((), (), s32[]{:S(2)}) async-start(), calls=%async_computation.12 | async-start | bytes 327680 | tf_op jit(solution)/shard_map/while/body/eval_jaxpr/reduce_scatter | solution.py:218
  1783.5 31.8 %reduce-scatter.9.cloned.1.call-start = ((), (), s32[]{:S(2)}) async-start(), calls=%async_computation.12 | async-start | bytes 327680 | tf_op jit(solution)/shard_map/while/body/eval_jaxpr/reduce_scatter | solution.py:218
  1815.2 31.8 %reduce-scatter.9.cloned.1.call-start = ((), (), s32[]{:S(2)}) async-start(), calls=%async_computation.12 | async-start | bytes 327680 | tf_op jit(solution)/shard_map/while/body/eval_jaxpr/reduce_scatter | solution.py:218
  1847.0 31.8 %reduce-scatter.9.cloned.1.call-start = ((), (), s32[]{:S(2)}) async-start(), calls=%async_computation.12 | async-start | bytes 327680 | tf_op jit(solution)/shard_map/while/body/eval_jaxpr/reduce_scatter | solution.py:218
  1878.8 31.8 %reduce-scatter.9.cloned.1.call-start = ((), (), s32[]{:S(2)}) async-start(), calls=%async_computation.12 | async-start | bytes 327680 | tf_op jit(solution)/shard_map/while/body/eval_jaxpr/reduce_scatter | solution.py:218
  1910.6 31.8 %reduce-scatter.9.cloned.1.call-start = ((), (), s32[]{:S(2)}) async-start(), calls=%async_computation.12 | async-start | bytes 327680 | tf_op jit(solution)/shard_map/while/body/eval_jaxpr/reduce_scatter | solution.py:218
  1942.4 31.8 %reduce-scatter.9.cloned.1.call-start = ((), (), s32[]{:S(2)}) async-start(), calls=%async_computation.12 | async-start | bytes 327680 | tf_op jit(solution)/shard_map/while/body/eval_jaxpr/reduce_scatter | solution.py:218
  1974.3 31.9 %reduce-scatter.9.cloned.1.call-start = ((), (), s32[]{:S(2)}) async-start(), calls=%async_computation.12 | async-start | bytes 327680 | tf_op jit(solution)/shard_map/while/body/eval_jaxpr/reduce_scatter | solution.py:218
  2006.1 31.8 %reduce-scatter.9.cloned.1.call-start = ((), (), s32[]{:S(2)}) async-start(), calls=%async_computation.12 | async-start | bytes 327680 | tf_op jit(solution)/shard_map/while/body/eval_jaxpr/reduce_scatter | solution.py:218
  2037.9 31.8 %reduce-scatter.9.cloned.1.call-start = ((), (), s32[]{:S(2)}) async-start(), calls=%async_computation.12 | async-start | bytes 327680 | tf_op jit(solution)/shard_map/while/body/eval_jaxpr/reduce_scatter | solution.py:218
  2069.7 31.8 %reduce-scatter.9.cloned.1.call-start = ((), (), s32[]{:S(2)}) async-start(), calls=%async_computation.12 | async-start | bytes 327680 | tf_op jit(solution)/shard_map/while/body/eval_jaxpr/reduce_scatter | solution.py:218
  2101.5 31.8 %reduce-scatter.9.cloned.1.call-start = ((), (), s32[]{:S(2)}) async-start(), calls=%async_computation.12 | async-start | bytes 327680 | tf_op jit(solution)/shard_map/while/body/eval_jaxpr/reduce_scatter | solution.py:218
  2133.3 31.8 %reduce-scatter.9.cloned.1.call-start = ((), (), s32[]{:S(2)}) async-start(), calls=%async_computation.12 | async-start | bytes 327680 | tf_op jit(solution)/shard_map/while/body/eval_jaxpr/reduce_scatter | solution.py:218
  2165.2 31.8 %reduce-scatter.9.cloned.1.call-start = ((), (), s32[]{:S(2)}) async-start(), calls=%async_computation.12 | async-start | bytes 327680 | tf_op jit(solution)/shard_map/while/body/eval_jaxpr/reduce_scatter | solution.py:218
  2197.0 31.8 %reduce-scatter.9.cloned.1.call-start = ((), (), s32[]{:S(2)}) async-start(), calls=%async_computation.12 | async-start | bytes 327680 | tf_op jit(solution)/shard_map/while/body/eval_jaxpr/reduce_scatter | solution.py:218
  2228.8 31.8 %reduce-scatter.9.cloned.1.call-start = ((), (), s32[]{:S(2)}) async-start(), calls=%async_computation.12 | async-start | bytes 327680 | tf_op jit(solution)/shard_map/while/body/eval_jaxpr/reduce_scatter | solution.py:218
  2260.6 31.8 %reduce-scatter.9.cloned.1.call-start = ((), (), s32[]{:S(2)}) async-start(), calls=%async_computation.12 | async-start | bytes 327680 | tf_op jit(solution)/shard_map/while/body/eval_jaxpr/reduce_scatter | solution.py:218
  2292.4 31.8 %reduce-scatter.9.cloned.1.call-start = ((), (), s32[]{:S(2)}) async-start(), calls=%async_computation.12 | async-start | bytes 327680 | tf_op jit(solution)/shard_map/while/body/eval_jaxpr/reduce_scatter | solution.py:218
  2324.2 31.8 %reduce-scatter.9.cloned.1.call-start = ((), (), s32[]{:S(2)}) async-start(), calls=%async_computation.12 | async-start | bytes 327680 | tf_op jit(solution)/shard_map/while/body/eval_jaxpr/reduce_scatter | solution.py:218
  2356.0 31.8 %reduce-scatter.9.cloned.1.call-start = ((), (), s32[]{:S(2)}) async-start(), calls=%async_computation.12 | async-start | bytes 327680 | tf_op jit(solution)/shard_map/while/body/eval_jaxpr/reduce_scatter | solution.py:218
  2387.8 31.8 %reduce-scatter.9.cloned.1.call-start = ((), (), s32[]{:S(2)}) async-start(), calls=%async_computation.12 | async-start | bytes 327680 | tf_op jit(solution)/shard_map/while/body/eval_jaxpr/reduce_scatter | solution.py:218
  2419.6 31.8 %reduce-scatter.9.cloned.1.call-start = ((), (), s32[]{:S(2)}) async-start(), calls=%async_computation.12 | async-start | bytes 327680 | tf_op jit(solution)/shard_map/while/body/eval_jaxpr/reduce_scatter | solution.py:218
  2451.4 31.8 %reduce-scatter.9.cloned.1.call-start = ((), (), s32[]{:S(2)}) async-start(), calls=%async_computation.12 | async-start | bytes 327680 | tf_op jit(solution)/shard_map/while/body/eval_jaxpr/reduce_scatter | solution.py:218
  2483.2 31.8 %reduce-scatter.9.cloned.1.call-start = ((), (), s32[]{:S(2)}) async-start(), calls=%async_computation.12 | async-start | bytes 327680 | tf_op jit(solution)/shard_map/while/body/eval_jaxpr/reduce_scatter | solution.py:218
  2515.1 84.6 %reduce-scatter.5.cloned.1.call-start = ((), (), s32[]{:S(2)}) async-start(), calls=%async_computation.8 | async-start | bytes 5734400 | tf_op jit(solution)/shard_map/reduce_scatter | solution.py:206
  2515.8 161.2 %all-reduce.13.cloned.1.call-start = ((), (), s32[]{:S(2)}) async-start(), calls=%async_computation.11 | async-start | bytes 5562368
  2609.8 198.8 %all-reduce.11.cloned.1.call-start = ((), (), s32[]{:S(2)}) async-start(), calls=%async_computation.7 | async-start | bytes 573440 | tf_op jit(solution)/shard_map/psum | solution.py:291
  2615.8 226.9 %all-gather.7.cloned.1.call-start = ((), (), s32[]{:S(2)}) async-start(), calls=%async_computation.10 | async-start | bytes 3128832 | tf_op jit(solution)/shard_map/all_gather | solution.py:287
  2679.1 372.4 %reduce-scatter.7.cloned.1.call-start = ((), (), s32[]{:S(2)}) async-start(), calls=%async_computation.9 | async-start | bytes 37748736 | tf_op jit(solution)/shard_map/reduce_scatter | solution.py:253
  (94 other events, 1264.7 us)
Sparse Core Ops, SparseCore 0:
  10.1 52.8 all-gather.4
  1120.6 20.7 reduce-scatter.10
  1176.7 17.3 reduce-scatter.10
  1203.1 17.3 reduce-scatter.10
  1229.5 17.3 reduce-scatter.10
  1255.9 17.3 reduce-scatter.10
  1282.3 17.3 reduce-scatter.10
  1308.8 17.3 reduce-scatter.10
  1335.2 17.3 reduce-scatter.10
  1361.6 17.3 reduce-scatter.10
  1388.0 17.3 reduce-scatter.10
  1414.4 17.3 reduce-scatter.10
  1440.8 17.3 reduce-scatter.10
  1467.2 17.3 reduce-scatter.10
  1493.6 17.3 reduce-scatter.10
  1520.0 17.3 reduce-scatter.10
  1546.4 17.3 reduce-scatter.10
  1572.8 17.3 reduce-scatter.10
  1599.2 17.3 reduce-scatter.10
  1765.6 17.7 reduce-scatter.8
  1797.3 17.8 reduce-scatter.8
  1829.1 17.8 reduce-scatter.8
  1860.9 17.8 reduce-scatter.8
  1892.7 17.8 reduce-scatter.8
  1924.5 17.8 reduce-scatter.8
  1956.3 17.8 reduce-scatter.8
  1988.1 17.9 reduce-scatter.8
  2020.0 17.8 reduce-scatter.8
  2051.8 17.8 reduce-scatter.8
  2083.6 17.8 reduce-scatter.8
  2115.4 17.8 reduce-scatter.8
  2147.2 17.9 reduce-scatter.8
  2179.1 17.8 reduce-scatter.8
  2210.9 17.8 reduce-scatter.8
  2242.7 17.8 reduce-scatter.8
  2274.5 17.8 reduce-scatter.8
  2306.3 17.8 reduce-scatter.8
  2338.1 17.8 reduce-scatter.8
  2369.9 17.8 reduce-scatter.8
  2401.7 17.8 reduce-scatter.8
  2433.5 17.8 reduce-scatter.8
  2465.3 17.8 reduce-scatter.8
  2497.1 17.8 reduce-scatter.8
  2518.2 81.3 reduce-scatter.4
  2609.9 67.0 all-reduce.12
  2683.2 125.3 all-reduce.10
  2810.9 31.7 all-gather.6
  2846.3 205.2 reduce-scatter.6
  (6 shorter events, 103.8 us)
